TPU v7x, 32 devices: a whole 2x2x4 slice. The times are simulated.
32 devices in a mesh: inst: 2 (over core), lon: 16 (over z, y, x).
Axes of the slice: x: 2, y: 2, z: 4, core: 2. Of those that a mesh axis runs over, the one named last changes fastest.
Arguments:
- obs_x: bfloat16 [384, 128, 256], P(('inst', 'lon')), may hold values from -6 to 6
- obs_cot: bfloat16 [384, 128, 256], P(('inst', 'lon')), may hold values from -6 to 6
- tile_window: int32 [384, 2], P(('inst', 'lon')), may hold values from 0 to 179, as said below
- point_mask: int32 [384, 128], P(('inst', 'lon')), may hold values from 0 to 1, as said below
- band_counts: int32 [32], P(('inst', 'lon')), may hold values from 1 to 12, as said below
- latents: bfloat16 [64, 184, 256], P('lon'), may hold values from -6 to 6
- w_query: bfloat16 [256, 128], replicated, may hold values from -3 to 3
- w_key: bfloat16 [256, 128], replicated, may hold values from -0.375 to 0.375
- w_value: bfloat16 [256, 128], replicated, may hold values from -0.375 to 0.375
- w_out: bfloat16 [128, 256], replicated, may hold values from -0.5 to 0.5
Outputs:
- decoded: bfloat16 [384, 128, 256], P(('inst', 'lon'))
- obs_grad: bfloat16 [384, 128, 256], P(('inst', 'lon'))
- latent_grad: float32 [64, 184, 256], P('lon')
- query_grad: float32 [256, 128], replicated
- key_grad: float32 [256, 128], replicated
- value_grad: float32 [256, 128], replicated
- out_grad: float32 [128, 256], replicated
Inputs may be any that keep to these rules, and one draw needn't show every extreme that they name: `tile_window`: column 0 is the first longitude column of the tile's window; the window's centre column (column 2) mod 64 is one of the 4 columns of the band that holds the tile. Column 1 is the window's first latitude row, at most 179. `point_mask`: in each tile the live slots come first, and half or more of the slots are live. `band_counts`: one entry equals 12.
All inputs are finite; a program needn't handle non-finite values.
Results may differ from a plain program's by a relative error of at most 0.007.
The roundings to bfloat16 on the way count: a program that leaves them out, or rounds other values in their place, can miss the bound.
Values may be sent and summed in bfloat16 or wider, within the bound.
A program may use at most 64 MiB of HBM per device.

v0:
```python
import math
import jax
import jax.numpy as jnp
from jax import lax
from jax.sharding import PartitionSpec as P

HEADS = 4
REACH = 2
softcap = 30.0


def with_halo(block, sides, width):
    for axis, dim in sides:
        count = lax.axis_size(axis)
        forward = [(i, i + 1) for i in range(count - 1)]
        forward.append((count - 1, 0))
        backward = [(target, source) for source, target in forward]
        low = lax.ppermute(
            lax.slice_in_dim(block, block.shape[dim] - width, None, axis=dim), axis, forward
        )
        high = lax.ppermute(lax.slice_in_dim(block, 0, width, axis=dim), axis, backward)
        block = jnp.concatenate([low, block, high], axis=dim)
    return block


def passed_along(block, axis, distance):
    devices = range(lax.axis_size(axis))
    route = [((i - distance) % len(devices), i) for i in devices]
    return lax.ppermute(block, axis, route)


def split_products(grad, w_pair, flat_latents):
    grad_high = grad.astype(jnp.bfloat16)
    grad_low = (grad - grad_high.astype(jnp.float32)).astype(jnp.bfloat16)
    by_rows = (((1,), (1,)), ((), ()))
    by_cols = (((0,), (0,)), ((), ()))
    latent_part = lax.dot_general(
        grad_high, w_pair, by_rows, preferred_element_type=jnp.float32
    ) + lax.dot_general(grad_low, w_pair, by_rows, preferred_element_type=jnp.float32)
    pair_weight = lax.dot_general(
        flat_latents, grad_high, by_cols, preferred_element_type=jnp.float32
    ) + lax.dot_general(flat_latents, grad_low, by_cols, preferred_element_type=jnp.float32)
    return (latent_part, pair_weight)


def attend(obs_x, obs_cot, live_points, windows, w_query, w_out):
    n_tiles, tile_len, model_width = obs_x.shape
    attn_width = w_query.shape[1]
    head_size = attn_width // HEADS
    score_scale = 1.0 / math.sqrt(head_size)
    flat_x = obs_x.reshape(-1, model_width)
    queries = jnp.dot(flat_x, w_query, preferred_element_type=jnp.float32).astype(jnp.bfloat16)
    query_heads = queries.reshape(n_tiles, tile_len, HEADS, head_size)
    win_keys = windows[:, :, :attn_width].reshape(n_tiles, -1, HEADS, head_size)
    win_values = windows[:, :, attn_width:].reshape(n_tiles, -1, HEADS, head_size)
    raw_scores = (
        jnp.einsum("nqhd,nkhd->nhqk", query_heads, win_keys, preferred_element_type=jnp.float32)
        * score_scale
    )
    capped = softcap * jnp.tanh(raw_scores / softcap)
    weights = jnp.exp(capped)
    probs = weights / jnp.sum(weights, axis=-1, keepdims=True)
    probs_b = probs.astype(jnp.bfloat16)
    attended = jnp.einsum(
        "nhqk,nkhd->nqhd", probs_b, win_values, preferred_element_type=jnp.float32
    )
    attended = attended.astype(jnp.bfloat16).reshape(-1, attn_width)
    projected = jnp.dot(attended, w_out, preferred_element_type=jnp.float32).reshape(
        n_tiles, tile_len, model_width
    )
    decoded = (obs_x.astype(jnp.float32) + live_points[:, :, None] * projected).astype(jnp.bfloat16)
    masked = obs_cot * live_points.astype(jnp.bfloat16)[:, :, None]
    flat_cot = masked.reshape(-1, model_width)
    out_grad = jnp.dot(attended.T, flat_cot, preferred_element_type=jnp.float32)
    attended_grad = jnp.dot(flat_cot, w_out.T, preferred_element_type=jnp.float32).astype(
        jnp.bfloat16
    )
    attended_grad = attended_grad.reshape(n_tiles, tile_len, HEADS, head_size)
    prob_grad = jnp.einsum(
        "nqhd,nkhd->nhqk", attended_grad, win_values, preferred_element_type=jnp.float32
    )
    row_inner = jnp.sum(probs * prob_grad, axis=-1, keepdims=True)
    score_grad = (
        probs * (prob_grad - row_inner) * (1.0 - (capped / softcap) ** 2) * score_scale
    ).astype(jnp.bfloat16)
    query_part = jnp.einsum(
        "nhqk,nkhd->nqhd", score_grad, win_keys, preferred_element_type=jnp.float32
    )
    query_part = query_part.astype(jnp.bfloat16).reshape(-1, attn_width)
    key_part = jnp.einsum(
        "nhqk,nqhd->nkhd", score_grad, query_heads, preferred_element_type=jnp.float32
    )
    value_part = jnp.einsum(
        "nhqk,nqhd->nkhd", probs_b, attended_grad, preferred_element_type=jnp.float32
    )
    window_grad = jnp.concatenate(
        [key_part.reshape(n_tiles, -1, attn_width), value_part.reshape(n_tiles, -1, attn_width)],
        axis=-1,
    )
    obs_grad = obs_cot.astype(jnp.float32).reshape(-1, model_width) + jnp.dot(
        query_part, w_query.T, preferred_element_type=jnp.float32
    )
    obs_grad = obs_grad.astype(jnp.bfloat16).reshape(n_tiles, tile_len, model_width)
    query_grad = jnp.dot(flat_x.T, query_part, preferred_element_type=jnp.float32)
    return (decoded, obs_grad, window_grad, query_grad, out_grad)


def shards(
    obs_x, obs_cot, tile_window, point_mask, band_counts, latents, w_query, w_key, w_value, w_out
):
    band_cols, lat_rows, model_width = latents.shape
    attn_width = w_query.shape[1]
    lon_cols = band_cols * lax.axis_size("lon")
    window = 2 * REACH + 1
    w_pair = jnp.concatenate([w_key, w_value], axis=1)
    own_pairs = jnp.dot(
        latents.reshape(-1, model_width), w_pair, preferred_element_type=jnp.float32
    ).astype(jnp.bfloat16)
    own_pairs = own_pairs.reshape(band_cols, lat_rows, 2 * attn_width)
    wide_pairs = with_halo(own_pairs, (("lon", 0),), REACH).reshape(-1, 2 * attn_width)
    band_first = lax.axis_index("lon") * band_cols
    offsets = jnp.arange(window, dtype=jnp.int32)
    starts = (tile_window[:, 0:1] - band_first + REACH) % lon_cols + offsets[None, :]
    lat_index = tile_window[:, 1:2] + offsets[None, :]
    key_index = (starts[:, :, None] * lat_rows + lat_index[:, None, :]).reshape(-1, window * window)
    windows = jnp.take(wide_pairs, key_index, axis=0)
    local_tile = jnp.arange(obs_x.shape[0], dtype=jnp.int32)
    live_points = (
        point_mask.astype(jnp.float32) * (local_tile < band_counts[0]).astype(jnp.float32)[:, None]
    )
    decoded, obs_grad, window_grad, query_grad, out_grad = attend(
        obs_x, obs_cot, live_points, windows, w_query, w_out
    )
    wide_cols = band_cols + 2 * REACH
    pair_grad = jnp.zeros((wide_cols * lat_rows, 2 * attn_width), jnp.float32)
    pair_grad = pair_grad.at[key_index.reshape(-1)].add(window_grad.reshape(-1, 2 * attn_width))
    pair_grad = pair_grad.reshape(wide_cols, lat_rows, 2 * attn_width)
    from_right = passed_along(pair_grad[:REACH].astype(jnp.bfloat16), "lon", -1).astype(jnp.float32)
    from_left = passed_along(pair_grad[band_cols + REACH :].astype(jnp.bfloat16), "lon", 1).astype(
        jnp.float32
    )
    own_grad = pair_grad[REACH : band_cols + REACH]
    own_grad = own_grad.at[:REACH].add(from_left)
    own_grad = own_grad.at[band_cols - REACH :].add(from_right)
    flat_grad = own_grad.reshape(-1, 2 * attn_width)
    flat_latents = latents.reshape(-1, model_width)
    latent_part, pair_weight = split_products(flat_grad, w_pair, flat_latents)
    latent_grad = lax.psum(latent_part, "inst")
    query_grad, out_grad, pair_weight = lax.psum(
        (query_grad, out_grad, pair_weight), ("inst", "lon")
    )
    return (
        decoded,
        obs_grad,
        latent_grad.reshape(band_cols, lat_rows, model_width),
        query_grad,
        pair_weight[:, :attn_width],
        pair_weight[:, attn_width:],
        out_grad,
    )


def solution(mesh):
    placed = (
        P(("inst", "lon"), None, None),
        P(("inst", "lon"), None, None),
        P(("inst", "lon"), None),
        P(("inst", "lon"), None),
        P(("inst", "lon")),
        P("lon", None, None),
        P(),
        P(),
        P(),
        P(),
    )
    return jax.shard_map(
        shards,
        mesh=mesh,
        in_specs=placed,
        out_specs=(
            P(("inst", "lon"), None, None),
            P(("inst", "lon"), None, None),
            P("lon", None, None),
            P(),
            P(),
            P(),
            P(),
        ),
        check_vma=False,
    )
```

profile of v0, /device:TPU:0, one launch (start us, length us, event | category | flops | bytes accessed | tf_op | source)
XLA Modules:
  0.0 227.1 jit_solution(15239581388625097601)
XLA Ops:
  7.3 0.9 constant_dynamic-update-slice_fusion.1
  8.2 0.9 constant_dynamic-update-slice_fusion
  9.1 0.3 convolution_convert_fusion.4
  9.3 0.8 fusion.62
  10.1 7.0 %collective-permute-start.1 = (bf16[2,184,256]{2,1,0:T(8,128)(2,1)}, bf16[2,184,256]{2,1,0:T(8,128)(2,1)}, u32[]{:S(2)}, u32[]{:S(2)}) collective-permute-start(bf16[2,184,256]{2,1,0:T(8,128)(2,1)} %bitcast.7), channel_id=1, source_target_pairs={{1,0},{2,1},{3,2},{4,3},{5,4},{6,5},{7,6},{8,7},{9,8},{10,9},{11,1... | collective-permute-start | bytes 565256 | tf_op jit(solution)/shard_map/ppermute | solution.py:21
  17.2 0.1 broadcast_add_fusion
  17.2 0.1 add.178
  18.2 0.1 copy.52
  18.3 0.1 copy.29
  18.4 0.1 copy.53
  18.5 0.1 copy.31
  18.6 0.1 reshape.286
  18.7 0.4 convolution_convert_fusion.1
  19.1 0.2 copy.33
  19.3 1.1 reshape.270
  20.4 0.7 fusion.60
  21.1 1.4 broadcast_multiply_fusion
  22.5 1.1 convolution_convert_fusion
  23.6 1.2 copy.37
  24.7 1.1 reshape.275
  25.8 0.6 fusion.45
  26.4 0.7 collective-permute-done
  27.2 1.1 pad_maximum_fusion
  28.3 2.0 gather_fusion
  30.4 0.1 broadcast_select_fusion
  30.5 1.0 copy.54
  31.5 0.3 copy.32
  31.8 1.2 fusion.36
  33.0 0.5 fusion.19
  33.5 0.9 copy-done.23
  34.3 1.1 convolution_convert_fusion.3
  35.4 3.2 %fusion.8 = bf16[12,128,4,32]{1,3,2,0:T(8,128)(2,1)} fusion(bf16[12,25,4,32]{1,3,2,0:T(8,128)(2,1)S(1)} %bitcast.118, f32[12,4,128,25]{2,3,1,0:T(8,128)} %fusion.36, f32[12,4,128,25]{2,3,1,0:T(8,128)} %copy-done.23, f32[12,4,128]{2,1,0:T(4,128)S(1)} %get-tuple-element.62), kind=kOutput, calls=%fused_computation.21 | convolution fusion | flops 11876376 | bytes 1723392 | tf_op jit(solution)/shard_map/nhqk,nkhd->nqhd/dot_general | solution.py:86
  38.6 2.7 %convolution_bitcast_fusion.1 = f32[12,25,4,32]{1,3,2,0:T(8,128)S(1)} fusion(f32[12,4,128,25]{2,3,1,0:T(8,128)} %fusion.36, f32[12,4,128,25]{2,3,1,0:T(8,128)} %copy-done.23, bf16[12,128,4,32]{1,0,3,2:T(8,128)(2,1)} %reshape.270, f32[12,4,128]{2,1,0:T(4,128)S(1)} %get-tuple-element.62), kind=kOutput, calls=%fused_computation.12 | convolution fusion | flops 11679768 | bytes 1800192 | tf_op jit(solution)/shard_map/nhqk,nqhd->nkhd/dot_general | solution.py:90
  41.3 2.4 %convolution_bitcast_fusion = f32[12,25,4,32]{1,3,2,0:T(8,128)} fusion(bf16[12,128,4,32]{1,0,3,2:T(8,128)(2,1)S(1)} %copy-done.6, f32[12,4,128,25]{2,3,1,0:T(8,128)} %copy-done.23, f32[12,4,128]{2,1,0:T(4,128)S(1)} %get-tuple-element.62), kind=kOutput, calls=%fused_computation.11 | convolution fusion | flops 10291200 | bytes 1185792 | tf_op jit(solution)/shard_map/nhqk,nqhd->nkhd/dot_general | solution.py:93
  43.6 1.5 copy.45
  45.1 1.0 concatenate.21
  46.1 0.4 copy.43
  46.4 1.0 concatenate.20
  47.4 3.0 %scatter_custom_fusion = f32[1472,256]{1,0:T(8,128)S(1)} fusion(s32[300]{0:T(512)} %fusion.45, f32[]{:T(128)} %constant.106.clone.1, f32[300,128]{1,0:T(8,128)} %concatenate.21, f32[]{:T(128)} %constant.116, f32[300,128]{1,0:T(8,128)} %concatenate.20), kind=kCustom, calls=%fused_computation.37 | custom fusion | flops 153600 | bytes 1819648 | tf_op jit(solution)/shard_map/scatter-add | solution.py:136
  50.4 0.1 convert.5
  50.5 1.0 copy-done.1
  51.6 0.2 copy-done.12
  51.7 0.3 copy.41
  52.0 0.9 convolution_bitcast_fusion.4
  52.9 0.3 copy.46
  53.3 5.6 %collective-permute-start.3 = (bf16[2,184,256]{2,1,0:T(8,128)(2,1)S(1)}, bf16[2,184,256]{2,1,0:T(8,128)(2,1)S(1)}, u32[]{:S(2)}, u32[]{:S(2)}) collective-permute-start(bf16[2,184,256]{2,1,0:T(8,128)(2,1)S(1)} %bitcast.119), channel_id=1, source_target_pairs={{1,0},{2,1},{3,2},{4,3},{5,4},{6,5},{7,6},{8,7},{9,8},{10,9},{11,1... | collective-permute-start | bytes 565256 | tf_op jit(solution)/shard_map/ppermute | solution.py:29
  58.9 0.9 fusion.20
  59.9 2.6 %collective-permute-done.2 = bf16[2,184,256]{2,1,0:T(8,128)(2,1)S(1)} collective-permute-done((bf16[2,184,256]{2,1,0:T(8,128)(2,1)S(1)}, bf16[2,184,256]{2,1,0:T(8,128)(2,1)S(1)}, u32[]{:S(2)}, u32[]{:S(2)}) %collective-permute-start.2) | collective-permute-done | bytes 188448 | tf_op jit(solution)/shard_map/ppermute | solution.py:29
  62.5 0.1 fusion.29
  62.6 0.3 convolution_bitcast_fusion.2
  62.9 0.8 fusion.15
  63.7 1.0 fusion.10
  64.8 0.3 fusion.65
  65.2 2.2 convolution_add_fusion.1
  67.5 1.3 fusion.1
  68.8 1.3 add_convert_fusion
  70.1 126.6 %all-reduce.6.cloned.1.call-done = (f32[256,128]{0,1:T(8,128)}, f32[256,256]{0,1:T(8,128)}, f32[128,256]{1,0:T(8,128)}) async-done(((f32[256,128]{0,1:T(8,128)}, f32[256,256]{0,1:T(8,128)}, f32[128,256]{1,0:T(8,128)}), (f32[256,128]{0,1:T(8,128)}, f32[256,256]{0,1:T(8,128)}, f32[128,256]{1,0:T(8,128)})) %all-reduce.6.cloned.1.call-update) | async-done | bytes 524304 | tf_op jit(solution)/shard_map/psum | solution.py:149
  196.7 1.7 copy.47
  198.4 1.0 fusion.63
  199.4 0.8 copy.49
  200.1 0.8 copy.48
  200.9 16.7 %all-reduce.4.cloned.1.call-done = f32[4,184,256]{2,1,0:T(8,128)} async-done(((f32[4,184,256]{2,1,0:T(8,128)}), f32[4,184,256]{2,1,0:T(8,128)}) %all-reduce.4.cloned.1.call-update) | async-done | bytes 753680 | tf_op jit(solution)/shard_map/psum | solution.py:148
  217.6 2.0 copy.87
  219.6 0.7 copy.88
  (69 shorter events, 0.7 us)
Async XLA Ops:
  7.2 1.9 copy-start
  7.2 9.9 %copy-start.22 = (s32[12,2]{0,1:T(2,128)S(1)}, s32[12,2]{0,1:T(2,128)}, u32[]{:S(2)}) copy-start(s32[12,2]{0,1:T(2,128)} %param.16) | copy-start | bytes 292
  7.2 11.5 %copy-start.15 = (bf16[256,128]{1,0:T(8,128)(2,1)S(1)}, bf16[256,128]{1,0:T(8,128)(2,1)}, u32[]{:S(2)}) copy-start(bf16[256,128]{1,0:T(8,128)(2,1)} %param.20) | copy-start | bytes 196612
  7.2 11.5 %copy-start.2 = (bf16[12,128,256]{2,1,0:T(8,128)(2,1)S(1)}, bf16[12,128,256]{2,1,0:T(8,128)(2,1)}, u32[]{:S(2)}) copy-start(bf16[12,128,256]{2,1,0:T(8,128)(2,1)} %param.14) | copy-start | bytes 2359300
  7.2 189.5 %all-reduce.6.cloned.1.call-start = ((), (), s32[]{:S(2)}) async-start(), calls=%async_computation.1 | async-start | bytes 1048576 | tf_op jit(solution)/shard_map/psum | solution.py:149
  9.1 10.0 %copy-start.7 = (bf16[256,256]{1,0:T(8,128)(2,1)}, bf16[256,256]{1,0:T(8,128)(2,1)S(1)}, u32[]{:S(2)}) copy-start(bf16[256,256]{1,0:T(8,128)(2,1)S(1)} %constant_dynamic-update-slice_fusion) | copy-start | bytes 393220
  10.1 16.3 %collective-permute-start.1 = (bf16[2,184,256]{2,1,0:T(8,128)(2,1)}, bf16[2,184,256]{2,1,0:T(8,128)(2,1)}, u32[]{:S(2)}, u32[]{:S(2)}) collective-permute-start(bf16[2,184,256]{2,1,0:T(8,128)(2,1)} %bitcast.7), channel_id=1, source_target_pairs={{1,0},{2,1},{3,2},{4,3},{5,4},{6,5},{7,6},{8,7},{9,8},{10,9},{11,1... | collective-permute-start | bytes 565256 | tf_op jit(solution)/shard_map/ppermute | solution.py:21
  17.1 10.1 %collective-permute-start = (bf16[2,184,256]{2,1,0:T(8,128)(2,1)}, bf16[2,184,256]{2,1,0:T(8,128)(2,1)}, u32[]{:S(2)}, u32[]{:S(2)}) collective-permute-start(bf16[2,184,256]{2,1,0:T(8,128)(2,1)} %bitcast.5), channel_id=1, source_target_pairs={{0,1},{1,2},{2,3},{3,4},{4,5},{5,6},{6,7},{7,8},{8,9},{9,10},{10,1... | collective-permute-start | bytes 565256 | tf_op jit(solution)/shard_map/ppermute | solution.py:18
  18.5 1.9 copy-start.21
  19.1 3.4 %copy-start.17 = (bf16[128,256]{1,0:T(8,128)(2,1)S(1)}, bf16[128,256]{1,0:T(8,128)(2,1)}, u32[]{:S(2)}) copy-start(bf16[128,256]{1,0:T(8,128)(2,1)} %param.23) | copy-start | bytes 196612
  30.3 1.5 copy-start.6
  30.5 2.5 %copy-start.11 = (bf16[12,128,4,32]{1,0,3,2:T(8,128)(2,1)S(1)}, bf16[12,128,4,32]{1,0,3,2:T(8,128)(2,1)}, u32[]{:S(2)}) copy-start(bf16[12,128,4,32]{1,0,3,2:T(8,128)(2,1)} %reshape.270) | copy-start | bytes 1179652
  31.8 1.2 copy-start.13
  33.5 0.9 copy-start.23
  34.3 1.1 copy-start.14
  50.4 1.1 copy-start.1
  50.4 1.3 copy-start.12
  50.5 2.4 %copy-start.9 = (bf16[12,4,32,128]{3,2,1,0:T(8,128)(2,1)S(1)}, bf16[12,4,32,128]{3,2,1,0:T(8,128)(2,1)}, u32[]{:S(2)}) copy-start(bf16[12,4,32,128]{3,2,1,0:T(8,128)(2,1)} %convolution_convert_fusion.3) | copy-start | bytes 1179652
  52.0 7.9 %copy-start.3 = (bf16[12,128,4,32]{1,0,3,2:T(8,128)(2,1)}, bf16[12,128,4,32]{1,0,3,2:T(8,128)(2,1)S(1)}, u32[]{:S(2)}) copy-start(bf16[12,128,4,32]{1,0,3,2:T(8,128)(2,1)S(1)} %copy.41) | copy-start | bytes 1179652
  52.9 9.6 %slice-start = ((f32[1472,256]{1,0:T(8,128)}), f32[368,256]{1,0:T(8,128)S(1)}, s32[]{:S(2)}) async-start(f32[1472,256]{1,0:T(8,128)} %copy-done.1), calls=%async_computation.2 | async-start | bytes 753664 | tf_op jit(solution)/shard_map/slice.60
  52.9 9.6 %slice-start.1 = ((f32[1472,256]{1,0:T(8,128)}), f32[736,256]{1,0:T(8,128)S(1)}, s32[]{:S(2)}) async-start(f32[1472,256]{1,0:T(8,128)} %copy-done.1), calls=%async_computation.3 | async-start | bytes 1507328 | tf_op jit(solution)/shard_map/slice | solution.py:142
  53.2 9.2 %collective-permute-start.2 = (bf16[2,184,256]{2,1,0:T(8,128)(2,1)S(1)}, bf16[2,184,256]{2,1,0:T(8,128)(2,1)S(1)}, u32[]{:S(2)}, u32[]{:S(2)}) collective-permute-start(bf16[2,184,256]{2,1,0:T(8,128)(2,1)S(1)} %bitcast.120), channel_id=1, source_target_pairs={{15,0},{0,1},{1,2},{2,3},{3,4},{4,5},{5,6},{6,7},{7,8},{8,9},{9,10... | collective-permute-start | bytes 565256 | tf_op jit(solution)/shard_map/ppermute | solution.py:29
  53.3 9.2 %collective-permute-start.3 = (bf16[2,184,256]{2,1,0:T(8,128)(2,1)S(1)}, bf16[2,184,256]{2,1,0:T(8,128)(2,1)S(1)}, u32[]{:S(2)}, u32[]{:S(2)}) collective-permute-start(bf16[2,184,256]{2,1,0:T(8,128)(2,1)S(1)} %bitcast.119), channel_id=1, source_target_pairs={{1,0},{2,1},{3,2},{4,3},{5,4},{6,5},{7,6},{8,7},{9,8},{10,9},{11,1... | collective-permute-start | bytes 565256 | tf_op jit(solution)/shard_map/ppermute | solution.py:29
  62.9 1.8 copy-start.8
  65.1 2.4 %copy-start.4 = (bf16[12,128,4,32]{1,0,3,2:T(8,128)(2,1)S(1)}, bf16[12,128,4,32]{1,0,3,2:T(8,128)(2,1)}, u32[]{:S(2)}) copy-start(bf16[12,128,4,32]{1,0,3,2:T(8,128)(2,1)} %copy-done.3) | copy-start | bytes 1179652
  65.1 2.4 %copy-start.5 = (bf16[12,128,256]{2,1,0:T(8,128)(2,1)S(1)}, bf16[12,128,256]{2,1,0:T(8,128)(2,1)}, u32[]{:S(2)}) copy-start(bf16[12,128,256]{2,1,0:T(8,128)(2,1)} %param.15) | copy-start | bytes 2359300
  65.1 2.4 %copy-start.16 = (bf16[256,128]{1,0:T(8,128)(2,1)S(1)}, bf16[256,128]{1,0:T(8,128)(2,1)}, u32[]{:S(2)}) copy-start(bf16[256,128]{1,0:T(8,128)(2,1)} %param.20) | copy-start | bytes 196612
  65.1 152.5 %all-reduce.4.cloned.1.call-start = ((), (), s32[]{:S(2)}) async-start(), calls=%async_computation | async-start | bytes 1507328 | tf_op jit(solution)/shard_map/psum | solution.py:148
  67.4 1.3 copy-start.10
  67.4 1.3 copy-start.18
  67.4 1.3 copy-start.20
  196.7 23.0 %copy-start.19 = (f32[128,256]{1,0:T(8,128)S(1)}, f32[128,256]{1,0:T(8,128)}, u32[]{:S(2)}) copy-start(f32[128,256]{1,0:T(8,128)} %get-tuple-element.72) | copy-start | bytes 393220
Sparse Core Ops, SparseCore 0:
  65.2 131.4 all-reduce.5
  199.6 17.9 all-reduce.3
where the time goes:
time: 228 us; the launch traced here: 227 us
  waiting for transfers between devices  147 us (64%)
  local copies, waits for them, and re-layouts  23.6 us (10%)
  matrix products  21 us (9%)
  between operations  15.1 us (7%)
  starting transfers between devices  12.7 us (6%)
  other arithmetic  8.08 us (4%)
    psum x1, waiting for transfers between devices, shards(): lax.psum((query_grad, out_grad, pair_weight), ('inst', 'lon'))  127 us
    psum x1, waiting for transfers between devices, shards(): latent_grad = lax.psum(latent_part, 'inst')  16.7 us
    unnamed x54, local copies, waits for them, and re-layouts  9 us
    ppermute x1, starting transfers between devices, with_halo(): lax.ppermute(lax.slice_in_dim(block, 0, width, axis=dim), axis, backward)  6.97 us
    ppermute x2, starting transfers between devices, passed_along(): return lax.ppermute(block, axis, route)  5.67 us
  transfers between devices with their start and end apart: 6, of which 4 were waited for; matrix products, arithmetic and copies ran while one was open for 8% of the time, Pallas kernels for 0%

commit v1 on v0

--- a/solution.py
+++ b/solution.py
@@ -145,7 +145,7 @@
     flat_grad = own_grad.reshape(-1, 2 * attn_width)
     flat_latents = latents.reshape(-1, model_width)
     latent_part, pair_weight = split_products(flat_grad, w_pair, flat_latents)
-    latent_grad = lax.psum(latent_part, "inst")
+    latent_grad = jnp.sum(lax.all_gather(latent_part, "inst"), axis=0)
     query_grad, out_grad, pair_weight = lax.psum(
         (query_grad, out_grad, pair_weight), ("inst", "lon")
     )

time: 228 us -> 213 us (0.934)
  waiting for transfers between devices: 147 us -> 130 us
  other arithmetic: 8.08 us -> 10.5 us
    psum x1 -> x0, waiting for transfers between devices: 16.7 us -> none  [shards(): latent_grad = lax.psum(latent_part, 'inst')]
    reduce_sum x0 -> x1, other arithmetic: none -> 2.43 us  [shards(): latent_grad = jnp.sum(lax.all_gather(latent_part, 'inst'), axis=0)]
    unnamed x54 -> x53, local copies, waits for them, and re-layouts: 9 us -> 6.93 us
  transfers between devices with their start and end apart: 6 -> 6, of which waited for: 4 -> 3; matrix products, arithmetic and copies ran while one was open for 8% -> 9% of each run, Pallas kernels for 0% -> 0%
where the time goes in v1:
time: 213 us; the launch traced here: 212 us
  waiting for transfers between devices  130 us (61%)
  local copies, waits for them, and re-layouts  21.5 us (10%)
  matrix products  21.1 us (10%)
  between operations  16.5 us (8%)
  starting transfers between devices  12.7 us (6%)
  other arithmetic  10.5 us (5%)
    psum x1, waiting for transfers between devices, shards(): lax.psum((query_grad, out_grad, pair_weight), ('inst', 'lon'))  127 us
    ppermute x1, starting transfers between devices, with_halo(): lax.ppermute(lax.slice_in_dim(block, 0, width, axis=dim), axis, backward)  6.97 us
    unnamed x53, local copies, waits for them, and re-layouts  6.93 us
    ppermute x2, starting transfers between devices, passed_along(): return lax.ppermute(block, axis, route)  5.67 us
  transfers between devices with their start and end apart: 6, of which 3 were waited for; matrix products, arithmetic and copies ran while one was open for 9% of the time, Pallas kernels for 0%

profile of v1, /device:TPU:0, one launch (start us, length us, event | category | flops | bytes accessed | tf_op | source)
XLA Modules:
  0.0 212.4 jit_solution(12087746813177318972)
XLA Ops:
  8.1 0.9 constant_dynamic-update-slice_fusion.1
  9.0 0.9 constant_dynamic-update-slice_fusion
  9.9 0.2 convolution_convert_fusion.4
  10.2 0.8 fusion.62
  10.9 7.0 %collective-permute-start.1 = (bf16[2,184,256]{2,1,0:T(8,128)(2,1)}, bf16[2,184,256]{2,1,0:T(8,128)(2,1)}, u32[]{:S(2)}, u32[]{:S(2)}) collective-permute-start(bf16[2,184,256]{2,1,0:T(8,128)(2,1)} %bitcast.7), channel_id=1, source_target_pairs={{1,0},{2,1},{3,2},{4,3},{5,4},{6,5},{7,6},{8,7},{9,8},{10,9},{11,1... | collective-permute-start | bytes 565256 | tf_op jit(solution)/shard_map/ppermute | solution.py:21
  17.9 0.1 iota_add_fusion
  18.0 0.1 broadcast_add_fusion
  18.1 0.1 add.176
  19.0 0.1 copy.52
  19.2 0.1 copy.29
  19.3 0.1 copy.53
  19.4 0.1 copy.31
  19.5 0.1 reshape.286
  19.6 0.4 convolution_convert_fusion.1
  20.0 0.2 copy.33
  20.1 1.1 reshape.270
  21.2 0.7 fusion.60
  21.9 1.4 broadcast_multiply_fusion
  23.3 1.1 convolution_convert_fusion
  24.4 1.2 copy.37
  25.6 1.1 reshape.275
  26.7 0.6 fusion.45
  27.3 0.7 collective-permute-done
  28.0 1.1 pad_maximum_fusion
  29.1 2.0 gather_fusion
  31.2 0.1 broadcast_select_fusion
  31.4 1.0 copy.54
  32.4 0.3 copy.32
  32.6 1.2 fusion.36
  33.9 0.5 fusion.19
  34.3 0.9 copy-done.23
  35.2 1.1 convolution_convert_fusion.3
  36.3 3.3 %fusion.8 = bf16[12,128,4,32]{1,3,2,0:T(8,128)(2,1)} fusion(bf16[12,25,4,32]{1,3,2,0:T(8,128)(2,1)S(1)} %bitcast.120, f32[12,4,128,25]{2,3,1,0:T(8,128)} %fusion.36, f32[12,4,128,25]{2,3,1,0:T(8,128)} %copy-done.23, f32[12,4,128]{2,1,0:T(4,128)S(1)} %get-tuple-element.62), kind=kOutput, calls=%fused_computation.21 | convolution fusion | flops 11876376 | bytes 1723392 | tf_op jit(solution)/shard_map/nhqk,nkhd->nqhd/dot_general | solution.py:86
  39.5 2.7 %convolution_bitcast_fusion.1 = f32[12,25,4,32]{1,3,2,0:T(8,128)S(1)} fusion(f32[12,4,128,25]{2,3,1,0:T(8,128)} %fusion.36, f32[12,4,128,25]{2,3,1,0:T(8,128)} %copy-done.23, bf16[12,128,4,32]{1,0,3,2:T(8,128)(2,1)} %reshape.270, f32[12,4,128]{2,1,0:T(4,128)S(1)} %get-tuple-element.62), kind=kOutput, calls=%fused_computation.12 | convolution fusion | flops 11679768 | bytes 1800192 | tf_op jit(solution)/shard_map/nhqk,nqhd->nkhd/dot_general | solution.py:90
  42.3 2.4 %convolution_bitcast_fusion = f32[12,25,4,32]{1,3,2,0:T(8,128)} fusion(bf16[12,128,4,32]{1,0,3,2:T(8,128)(2,1)S(1)} %copy-done.6, f32[12,4,128,25]{2,3,1,0:T(8,128)} %copy-done.23, f32[12,4,128]{2,1,0:T(4,128)S(1)} %get-tuple-element.62), kind=kOutput, calls=%fused_computation.11 | convolution fusion | flops 10291200 | bytes 1185792 | tf_op jit(solution)/shard_map/nhqk,nqhd->nkhd/dot_general | solution.py:93
  44.6 1.5 copy.45
  46.1 1.0 concatenate.21
  47.1 0.4 copy.43
  47.4 1.0 concatenate.20
  48.4 3.0 %scatter_custom_fusion = f32[1472,256]{1,0:T(8,128)S(1)} fusion(s32[300]{0:T(512)} %fusion.45, f32[]{:T(128)} %constant.106.clone.1, f32[300,128]{1,0:T(8,128)} %concatenate.21, f32[]{:T(128)} %constant.116, f32[300,128]{1,0:T(8,128)} %concatenate.20), kind=kCustom, calls=%fused_computation.37 | custom fusion | flops 153600 | bytes 1819648 | tf_op jit(solution)/shard_map/scatter-add | solution.py:136
  51.4 0.1 convert.5
  51.5 1.0 copy-done.1
  52.5 0.2 copy-done.12
  52.7 0.3 copy.41
  53.0 0.9 convolution_bitcast_fusion.4
  53.9 0.3 copy.46
  54.3 5.6 %collective-permute-start.3 = (bf16[2,184,256]{2,1,0:T(8,128)(2,1)S(1)}, bf16[2,184,256]{2,1,0:T(8,128)(2,1)S(1)}, u32[]{:S(2)}, u32[]{:S(2)}) collective-permute-start(bf16[2,184,256]{2,1,0:T(8,128)(2,1)S(1)} %bitcast.121), channel_id=1, source_target_pairs={{1,0},{2,1},{3,2},{4,3},{5,4},{6,5},{7,6},{8,7},{9,8},{10,9},{11,1... | collective-permute-start | bytes 565256 | tf_op jit(solution)/shard_map/ppermute | solution.py:29
  59.9 0.9 fusion.20
  60.8 2.6 %collective-permute-done.2 = bf16[2,184,256]{2,1,0:T(8,128)(2,1)S(1)} collective-permute-done((bf16[2,184,256]{2,1,0:T(8,128)(2,1)S(1)}, bf16[2,184,256]{2,1,0:T(8,128)(2,1)S(1)}, u32[]{:S(2)}, u32[]{:S(2)}) %collective-permute-start.2) | collective-permute-done | bytes 188448 | tf_op jit(solution)/shard_map/ppermute | solution.py:29
  63.5 0.1 fusion.29
  63.6 0.3 convolution_bitcast_fusion.2
  63.9 0.8 fusion.15
  64.7 1.0 fusion.10
  65.7 0.3 fusion.65
  66.1 2.2 %convolution_add_fusion.1 = f32[736,256]{1,0:T(8,128)} fusion(f32[736,256]{1,0:T(8,128)S(1)} %fusion.65, bf16[736,256]{1,0:T(8,128)(2,1)} %get-tuple-element.48, bf16[256,256]{1,0:T(8,128)(2,1)S(1)} %copy-done.8), kind=kOutput, calls=%fused_computation.16 | convolution fusion | flops 96657408 | bytes 2015232 | tf_op jit(solution)/shard_map/dot_general | solution.py:39
  68.4 1.3 fusion.1
  69.7 1.3 add_convert_fusion
  71.1 126.6 %all-reduce.3.cloned.1.call-done = (f32[256,128]{0,1:T(8,128)}, f32[256,256]{0,1:T(8,128)}, f32[128,256]{1,0:T(8,128)}) async-done(((f32[256,128]{0,1:T(8,128)}, f32[256,256]{0,1:T(8,128)}, f32[128,256]{1,0:T(8,128)}), (f32[256,128]{0,1:T(8,128)}, f32[256,256]{0,1:T(8,128)}, f32[128,256]{1,0:T(8,128)})) %all-reduce.3.cloned.1.call-update) | async-done | bytes 524304 | tf_op jit(solution)/shard_map/psum | solution.py:149
  197.7 1.7 copy.47
  199.3 1.0 fusion.63
  200.3 0.8 copy.49
  201.1 0.8 copy.48
  201.9 2.4 %reduce_sum.29 = f32[736,256]{1,0:T(8,128)} reduce(f32[2,736,256]{2,1,0:T(8,128)} %bitcast.116, f32[]{:T(128)} %constant.106.clone.1), dimensions={0}, to_apply=%region_3.4 | reduce | flops 188416 | bytes 2260996 | tf_op jit(solution)/shard_map/reduce_sum | solution.py:148
  204.3 0.7 copy.86
  (69 shorter events, 0.7 us)
Async XLA Ops:
  8.0 1.9 copy-start
  8.0 9.9 %copy-start.22 = (s32[12,2]{0,1:T(2,128)S(1)}, s32[12,2]{0,1:T(2,128)}, u32[]{:S(2)}) copy-start(s32[12,2]{0,1:T(2,128)} %param.16) | copy-start | bytes 292
  8.0 11.5 %copy-start.15 = (bf16[256,128]{1,0:T(8,128)(2,1)S(1)}, bf16[256,128]{1,0:T(8,128)(2,1)}, u32[]{:S(2)}) copy-start(bf16[256,128]{1,0:T(8,128)(2,1)} %param.20) | copy-start | bytes 196612
  8.0 11.5 %copy-start.2 = (bf16[12,128,256]{2,1,0:T(8,128)(2,1)S(1)}, bf16[12,128,256]{2,1,0:T(8,128)(2,1)}, u32[]{:S(2)}) copy-start(bf16[12,128,256]{2,1,0:T(8,128)(2,1)} %param.14) | copy-start | bytes 2359300
  8.0 189.6 %all-reduce.3.cloned.1.call-start = ((), (), s32[]{:S(2)}) async-start(), calls=%async_computation.1 | async-start | bytes 1048576 | tf_op jit(solution)/shard_map/psum | solution.py:149
  9.9 10.0 %copy-start.7 = (bf16[256,256]{1,0:T(8,128)(2,1)}, bf16[256,256]{1,0:T(8,128)(2,1)S(1)}, u32[]{:S(2)}) copy-start(bf16[256,256]{1,0:T(8,128)(2,1)S(1)} %constant_dynamic-update-slice_fusion) | copy-start | bytes 393220
  10.9 16.3 %collective-permute-start.1 = (bf16[2,184,256]{2,1,0:T(8,128)(2,1)}, bf16[2,184,256]{2,1,0:T(8,128)(2,1)}, u32[]{:S(2)}, u32[]{:S(2)}) collective-permute-start(bf16[2,184,256]{2,1,0:T(8,128)(2,1)} %bitcast.7), channel_id=1, source_target_pairs={{1,0},{2,1},{3,2},{4,3},{5,4},{6,5},{7,6},{8,7},{9,8},{10,9},{11,1... | collective-permute-start | bytes 565256 | tf_op jit(solution)/shard_map/ppermute | solution.py:21
  17.9 10.1 %collective-permute-start = (bf16[2,184,256]{2,1,0:T(8,128)(2,1)}, bf16[2,184,256]{2,1,0:T(8,128)(2,1)}, u32[]{:S(2)}, u32[]{:S(2)}) collective-permute-start(bf16[2,184,256]{2,1,0:T(8,128)(2,1)} %bitcast.5), channel_id=1, source_target_pairs={{0,1},{1,2},{2,3},{3,4},{4,5},{5,6},{6,7},{7,8},{8,9},{9,10},{10,1... | collective-permute-start | bytes 565256 | tf_op jit(solution)/shard_map/ppermute | solution.py:18
  19.4 1.9 copy-start.21
  19.9 3.4 %copy-start.17 = (bf16[128,256]{1,0:T(8,128)(2,1)S(1)}, bf16[128,256]{1,0:T(8,128)(2,1)}, u32[]{:S(2)}) copy-start(bf16[128,256]{1,0:T(8,128)(2,1)} %param.23) | copy-start | bytes 196612
  31.1 1.5 copy-start.6
  31.3 2.5 %copy-start.11 = (bf16[12,128,4,32]{1,0,3,2:T(8,128)(2,1)S(1)}, bf16[12,128,4,32]{1,0,3,2:T(8,128)(2,1)}, u32[]{:S(2)}) copy-start(bf16[12,128,4,32]{1,0,3,2:T(8,128)(2,1)} %reshape.270) | copy-start | bytes 1179652
  32.6 1.2 copy-start.13
  34.3 0.9 copy-start.23
  35.2 1.1 copy-start.14
  51.4 1.1 copy-start.1
  51.4 1.3 copy-start.12
  51.5 2.4 %copy-start.9 = (bf16[12,4,32,128]{3,2,1,0:T(8,128)(2,1)S(1)}, bf16[12,4,32,128]{3,2,1,0:T(8,128)(2,1)}, u32[]{:S(2)}) copy-start(bf16[12,4,32,128]{3,2,1,0:T(8,128)(2,1)} %convolution_convert_fusion.3) | copy-start | bytes 1179652
  53.0 7.9 %copy-start.3 = (bf16[12,128,4,32]{1,0,3,2:T(8,128)(2,1)}, bf16[12,128,4,32]{1,0,3,2:T(8,128)(2,1)S(1)}, u32[]{:S(2)}) copy-start(bf16[12,128,4,32]{1,0,3,2:T(8,128)(2,1)S(1)} %copy.41) | copy-start | bytes 1179652
  53.9 9.6 %slice-start = ((f32[1472,256]{1,0:T(8,128)}), f32[368,256]{1,0:T(8,128)S(1)}, s32[]{:S(2)}) async-start(f32[1472,256]{1,0:T(8,128)} %copy-done.1), calls=%async_computation.2 | async-start | bytes 753664 | tf_op jit(solution)/shard_map/slice.60
  53.9 9.6 %slice-start.1 = ((f32[1472,256]{1,0:T(8,128)}), f32[736,256]{1,0:T(8,128)S(1)}, s32[]{:S(2)}) async-start(f32[1472,256]{1,0:T(8,128)} %copy-done.1), calls=%async_computation.3 | async-start | bytes 1507328 | tf_op jit(solution)/shard_map/slice | solution.py:142
  54.2 9.2 %collective-permute-start.2 = (bf16[2,184,256]{2,1,0:T(8,128)(2,1)S(1)}, bf16[2,184,256]{2,1,0:T(8,128)(2,1)S(1)}, u32[]{:S(2)}, u32[]{:S(2)}) collective-permute-start(bf16[2,184,256]{2,1,0:T(8,128)(2,1)S(1)} %bitcast.122), channel_id=1, source_target_pairs={{15,0},{0,1},{1,2},{2,3},{3,4},{4,5},{5,6},{6,7},{7,8},{8,9},{9,10... | collective-permute-start | bytes 565256 | tf_op jit(solution)/shard_map/ppermute | solution.py:29
  54.3 9.2 %collective-permute-start.3 = (bf16[2,184,256]{2,1,0:T(8,128)(2,1)S(1)}, bf16[2,184,256]{2,1,0:T(8,128)(2,1)S(1)}, u32[]{:S(2)}, u32[]{:S(2)}) collective-permute-start(bf16[2,184,256]{2,1,0:T(8,128)(2,1)S(1)} %bitcast.121), channel_id=1, source_target_pairs={{1,0},{2,1},{3,2},{4,3},{5,4},{6,5},{7,6},{8,7},{9,8},{10,9},{11,1... | collective-permute-start | bytes 565256 | tf_op jit(solution)/shard_map/ppermute | solution.py:29
  63.9 1.8 copy-start.8
  66.1 2.4 %copy-start.4 = (bf16[12,128,4,32]{1,0,3,2:T(8,128)(2,1)S(1)}, bf16[12,128,4,32]{1,0,3,2:T(8,128)(2,1)}, u32[]{:S(2)}) copy-start(bf16[12,128,4,32]{1,0,3,2:T(8,128)(2,1)} %copy-done.3) | copy-start | bytes 1179652
  66.1 2.4 %copy-start.5 = (bf16[12,128,256]{2,1,0:T(8,128)(2,1)S(1)}, bf16[12,128,256]{2,1,0:T(8,128)(2,1)}, u32[]{:S(2)}) copy-start(bf16[12,128,256]{2,1,0:T(8,128)(2,1)} %param.15) | copy-start | bytes 2359300
  66.1 2.4 %copy-start.16 = (bf16[256,128]{1,0:T(8,128)(2,1)S(1)}, bf16[256,128]{1,0:T(8,128)(2,1)}, u32[]{:S(2)}) copy-start(bf16[256,128]{1,0:T(8,128)(2,1)} %param.20) | copy-start | bytes 196612
  66.1 135.8 %all-gather.3.cloned.1.call-start = ((), (), s32[]{:S(2)}) async-start(), calls=%async_computation | async-start | bytes 2260992 | tf_op jit(solution)/shard_map/all_gather | solution.py:148
  68.4 1.3 copy-start.10
  68.4 1.3 copy-start.18
  68.4 1.3 copy-start.20
  200.3 4.0 %copy-start.19 = (f32[128,256]{1,0:T(8,128)S(1)}, f32[128,256]{1,0:T(8,128)}, u32[]{:S(2)}) copy-start(f32[128,256]{1,0:T(8,128)} %get-tuple-element.72) | copy-start | bytes 393220
Sparse Core Ops, SparseCore 0:
  66.2 131.4 all-reduce.2
Sparse Core Ops, SparseCore 1:
  68.7 10.9 all-gather.2
